TPU v7x, 32 devices: a whole 2x2x4 slice. The times are simulated.
32 devices in a mesh: beam: 2 (over y), bin: 4 (over z), chan: 4 (over x, core).
Axes of the slice: x: 2, y: 2, z: 4, core: 2. Of those that a mesh axis runs over, the one named last changes fastest.
Arguments:
- spectra: bfloat16 [2, 8192, 1024], P(None, ('beam', 'chan', 'bin')), parts along dimension 1, may hold values from -6 to 6
- dm_trials: int32 [64], replicated, may hold values from 0 to 1023
- chan_delay: int32 [4096], replicated, may hold values from 0 to 32767
- template_bank: bfloat16 [2, 256, 256], replicated, may hold values from -0.25 to 0.25
- template_ids: int32 [128], replicated, may hold values from 0 to 255
Outputs:
- powers: bfloat16 [128, 128, 1024], P(('beam', 'chan'), None, 'bin'), parts along dimension 0
There are 2 independent parts, one for each index of `beam`. A program takes and returns all parts, laid end to end along the dimension named above; an argument that names none is the same for every part. Nothing has to cross between parts.
All inputs are finite; a program needn't handle non-finite values.
Results may differ from a plain program's by a relative error of at most 0.0095.
Values may be sent and summed in bfloat16 or wider, within the bound.
A program may use at most 64 MiB of HBM per device.

v0:
```python
import functools
import math

import jax
import jax.numpy as jnp
from jax import lax
from jax.experimental import pallas as pl
from jax.experimental.pallas import tpu as pltpu
from jax.sharding import PartitionSpec as P

EDGE = 128
LANES = 128
MESH = pl.DeviceIdType.MESH


def cos_sin(turns, samples):
    eighth = samples // 8
    quadrant = (turns + eighth) // (2 * eighth)
    rest = turns - quadrant * (2 * eighth)
    x = rest.astype(jnp.float32) * (2.0 * math.pi / samples)
    y = x * x
    c = 1.0 + y * (-0.5 + y * (1.0 / 24 + y * (-1.0 / 720 + y * (1.0 / 40320))))
    s = x * (1.0 + y * (-1.0 / 6 + y * (1.0 / 120 + y * (-1.0 / 5040 + y * (1.0 / 362880)))))
    swap = (quadrant & 1) == 1
    cos = jnp.where(swap, s, c)
    sin = jnp.where(swap, c, s)
    cos = jnp.where(((quadrant + 1) & 2) == 2, -cos, cos)
    sin = jnp.where((quadrant & 2) == 2, -sin, sin)
    return cos, sin


def take_lanes(x, index):
    return jnp.take_along_axis(x, index, axis=1, mode="promise_in_bounds")


def dedisperse_kernel(
    samples, scale, spec_ref, delay_ref, dm_ref, out_ref, send_ref, sum_ref, chan_recv, bin_recv,
    table_ref, even_ref, split_ref, merge_ref, prod_a, prod_b, chan_sems, bin_sems,
):
    bin_size = lax.axis_size("bin")
    chan_size = lax.axis_size("chan")
    my_bin = lax.axis_index("bin")
    my_chan = lax.axis_index("chan")
    chans = spec_ref.shape[1]
    bins = spec_ref.shape[2]
    half = samples // 2
    group = prod_a.shape[1] // 2
    blocks = group // LANES
    all_blocks = half // LANES
    groups, rows = send_ref.shape[:2]
    width = out_ref.shape[1]
    tile = LANES
    own = bins // bin_size
    tiles = own // tile
    padded = max(chans, LANES)

    def chan_at(offset):
        return lax.rem(my_chan + offset, chan_size)

    def bin_at(offset):
        return lax.rem(my_bin + offset, bin_size)

    barrier = pltpu.get_barrier_semaphore()

    def greet_chan(offset, _):
        pl.semaphore_signal(
            barrier, inc=1, device_id={"chan": chan_at(offset)}, device_id_type=MESH
        )
        return 0

    def greet_bin(offset, _):
        pl.semaphore_signal(barrier, inc=1, device_id={"bin": bin_at(offset)}, device_id_type=MESH)
        return 0

    lax.fori_loop(1, chan_size, greet_chan, 0)
    lax.fori_loop(1, bin_size, greet_bin, 0)

    if delay_ref.shape[1] == chans:
        delay = delay_ref[...]
    else:
        rank = lax.axis_index("chan") * bin_size + lax.axis_index("bin")
        delay = delay_ref[:, pl.ds(pl.multiple_of(rank * chans, LANES), chans)]
    if chans < padded:
        delay = jnp.concatenate([delay, jnp.zeros((1, padded - chans), jnp.int32)], 1)

    def rotations(count, stride):
        turns = lax.broadcasted_iota(jnp.int32, (count, padded), 0) * stride * delay
        return cos_sin(turns & (samples - 1), samples)

    fine_cos, fine_sin = rotations(8, 1)
    mid_cos, mid_sin = rotations(LANES // 8, 8)
    low_cos = jnp.concatenate(
        [fine_cos * mid_cos[a:a + 1] - fine_sin * mid_sin[a:a + 1] for a in range(LANES // 8)], 0
    ).T[:chans]
    low_sin = jnp.concatenate(
        [fine_sin * mid_cos[a:a + 1] + fine_cos * mid_sin[a:a + 1] for a in range(LANES // 8)], 0
    ).T[:chans]
    coarse_cos, coarse_sin = rotations(all_blocks + 8, LANES)
    fill_rows = jnp.zeros((LANES - all_blocks - 8, padded), jnp.float32)
    high_cos = jnp.concatenate([coarse_cos, fill_rows], 0).T[:chans]
    high_sin = jnp.concatenate([coarse_sin, fill_rows], 0).T[:chans]
    lane_ids = lax.broadcasted_iota(jnp.int32, (chans, LANES), 1)

    def fill(block, _):
        spread = jnp.full((chans, LANES), block, jnp.int32)
        block_cos = take_lanes(high_cos, spread)
        block_sin = take_lanes(high_sin, spread)
        at = pl.multiple_of(block * LANES, LANES)
        cos = low_cos * block_cos - low_sin * block_sin
        sin = low_sin * block_cos + low_cos * block_sin
        table_ref[:, pl.ds(at, LANES)] = cos.astype(jnp.bfloat16)
        table_ref[:, pl.ds(half + at, LANES)] = sin.astype(jnp.bfloat16)
        return 0

    lax.fori_loop(0, all_blocks, fill, 0)
    parity = take_lanes(high_cos, jnp.full((chans, LANES), all_blocks, jnp.int32))
    table_ref[:, half:half + LANES] = jnp.where(lane_ids == 0, parity, low_sin).astype(jnp.bfloat16)

    paired = half == group and tiles == 2 and half % (4 * LANES) == 0
    if paired:
        even_cos = low_cos * low_cos - low_sin * low_sin
        even_sin = 2.0 * low_sin * low_cos
        for block in range(all_blocks // 2):
            spread = jnp.full((chans, LANES), 2 * block, jnp.int32)
            block_cos = take_lanes(high_cos, spread)
            block_sin = take_lanes(high_sin, spread)
            at = block * LANES
            cos = even_cos * block_cos - even_sin * block_sin
            sin = even_sin * block_cos + even_cos * block_sin
            if block == 0:
                sin = jnp.where(lane_ids == 0, parity, sin)
            even_ref[:, at:at + LANES] = cos.astype(jnp.bfloat16)
            even_ref[:, half // 2 + at:half // 2 + at + LANES] = sin.astype(jnp.bfloat16)
        near = lax.broadcasted_iota(jnp.int32, (own, own), 0)
        far = lax.broadcasted_iota(jnp.int32, (own, own), 1)

        def source(spot):
            return jnp.where(spot < tile, 2 * spot + 1, 2 * (spot - tile))

        split_ref[...] = (near == source(far)).astype(jnp.float32).astype(jnp.bfloat16)
        merge_ref[...] = (far == source(near)).astype(jnp.float32).astype(jnp.bfloat16)

    lane = lax.broadcasted_iota(jnp.int32, (8, LANES), 1)
    is_real = (lane // (rows // 2)) % 2 == 0
    dm = jnp.broadcast_to(dm_ref[...], (8, dm_ref.shape[1]))
    dm = jnp.concatenate([dm] * (LANES // dm_ref.shape[1]), 1)
    dm = take_lanes(dm, (lane // rows) * (rows // 2) + lane % (rows // 2))

    def first_of(step):
        return pl.multiple_of(step * tile, tile)

    def multiply(step, g, prod_ref):
        at = pl.ds(first_of(step), tile)
        both = jnp.concatenate([spec_ref[0, :, at], spec_ref[1, :, at]], 1)
        for part in (0, 1):
            columns = pl.ds(pl.multiple_of(part * half + g * group, group), group)
            prod_ref[:, part * group:(part + 1) * group] = lax.dot_general(
                both, table_ref[:, columns], (((0,), (0,)), ((), ())),
                preferred_element_type=jnp.float32,
            )

    def turns_of(step, r):
        bin_ids = step * tile + r * 8 + lax.broadcasted_iota(jnp.int32, (8, LANES), 0)
        return (bin_ids * dm) & (samples - 1)

    def pick(turns, half, group, g, r, prod_ref, acc):
        folded = jnp.where(turns > half, 2 * half - turns, turns)
        index = folded & (half - 1)
        spot = index & (LANES - 1)
        which = index // LANES - g * (group // LANES)
        acc = list(acc)
        for b in range(group // LANES):
            hit = which == b
            for i, (part, table) in enumerate(((0, 0), (1, 1), (1, 0), (0, 1))):
                top = part * tile + r * 8
                left = table * group + b * LANES
                piece = take_lanes(prod_ref[top:top + 8, left:left + LANES], spot)
                acc[i] = piece if acc[i] is None else jnp.where(hit, piece, acc[i])
        return acc

    def finish(turns, half, acc):
        sign = jnp.where(turns > half, -1.0, jnp.where(turns == 0, 0.0, 1.0))
        a, b, a2, b2 = acc
        real = jnp.where(turns == half, b2, a + sign * b)
        imag = jnp.where(turns == half, b, a2 - sign * b2)
        return jnp.where(is_real, real, imag)

    def split_multiply(block, even, prod_ref):
        at = pl.ds(pl.multiple_of(block * own, LANES), own)
        chosen = split_ref[:, even * tile:(even + 1) * tile]
        both = jnp.concatenate(
            [
                jnp.dot(spec_ref[part, :, at], chosen, preferred_element_type=jnp.float32)
                for part in (0, 1)
            ],
            1,
        ).astype(jnp.bfloat16)
        size = 2 * half // (1 + even)
        prod_ref[:, :size] = lax.dot_general(
            both, (even_ref if even else table_ref)[...], (((0,), (0,)), ((), ())),
            preferred_element_type=jnp.float32,
        )

    def split_gather(block, even, prod_ref):
        pieces = []
        for r in range(tile // 8):
            spots = r * 8 + lax.broadcasted_iota(jnp.int32, (8, LANES), 0)
            bin_ids = block * own + 2 * spots + (1 - even)
            turns = ((bin_ids * dm) & (samples - 1)) >> even
            size = half >> even
            acc = pick(turns, size, size, 0, r, prod_ref, [None] * 4)
            pieces.append(finish(turns, size, acc))
        return pieces

    def put(step, pieces):
        block = jnp.concatenate(pieces, 0).T
        at = pl.ds(first_of(step), tile)
        send_ref[:, :, at] = block.reshape(groups, rows, tile).astype(send_ref.dtype)

    def block_at(p):
        return bin_at(p + 1)

    def compute(p):
        base = block_at(p) * tiles

        def one_tile(t, _):
            step = base + t

            def one_group(g, accs):
                multiply(step, g, prod_a)
                new = []
                for r in range(tile // 8):
                    new += pick(
                        turns_of(step, r), half, group, g, r, prod_a, accs[4 * r:4 * r + 4]
                    )
                return tuple(new)

            zero = jnp.zeros((8, LANES), jnp.float32)
            accs = lax.fori_loop(0, half // group, one_group, (zero,) * (4 * (tile // 8)))
            put(step, [
                finish(turns_of(step, r), half, accs[4 * r:4 * r + 4]) for r in range(tile // 8)
            ])
            return 0

        if paired:
            block = block_at(p)
            split_multiply(block, 1, prod_b)
            pieces = split_gather(block, 0, prod_a)
            split_multiply(block_at(jnp.minimum(p + 1, bin_size - 1)), 0, prod_a)
            pieces += split_gather(block, 1, prod_b)
            merged = lax.dot_general(
                jnp.concatenate(pieces, 0).astype(jnp.bfloat16), merge_ref[...],
                (((0,), (0,)), ((), ())), preferred_element_type=jnp.float32,
            )
            at = pl.ds(pl.multiple_of(block * own, LANES), own)
            send_ref[:, :, at] = merged.reshape(groups, rows, own).astype(send_ref.dtype)
        else:
            lax.fori_loop(0, tiles, one_tile, 0)

    def chan_copy(p, offset):
        at = pl.ds(pl.multiple_of(block_at(p) * own, LANES), own)
        return pltpu.make_async_remote_copy(
            src_ref=send_ref.at[chan_at(offset), :, at],
            dst_ref=chan_recv.at[chan_size - offset, :, at],
            send_sem=chan_sems.at[0, offset, p],
            recv_sem=chan_sems.at[1, chan_size - offset, p],
            device_id={"chan": chan_at(offset)},
            device_id_type=MESH,
        )

    def bin_copy(block, piece):
        to = block + (0, 1, -1)[piece]
        begin, size, land = ((0, own, EDGE), (own - EDGE, EDGE, 0), (0, EDGE, EDGE + own))[piece]
        offset = lax.rem(to - my_bin + bin_size, bin_size)
        slot = lax.rem(bin_size - offset, bin_size)
        return pltpu.make_async_remote_copy(
            src_ref=sum_ref.at[:, pl.ds(pl.multiple_of(EDGE + block * own + begin, LANES), size)],
            dst_ref=bin_recv.at[slot, :, land:land + size],
            send_sem=bin_sems.at[0, piece, offset],
            recv_sem=bin_sems.at[1, piece, slot],
            device_id={"bin": to},
            device_id_type=MESH,
        )

    def each_piece(block, act):
        for piece in range(3):
            to = block + (0, 1, -1)[piece]

            @pl.when((to >= 0) & (to < bin_size) & (to != my_bin))
            def _():
                act(bin_copy(block, piece))

    def forward(p):
        block = block_at(p)
        at = pl.multiple_of(block * own, LANES)
        for offset in range(1, chan_size):
            chan_copy(p, chan_size - offset).wait_recv()
        total = send_ref[my_chan, :, pl.ds(at, own)].astype(jnp.float32)
        for offset in range(1, chan_size):
            total += chan_recv[offset, :, pl.ds(at, own)].astype(jnp.float32)
        sum_ref[:, pl.ds(pl.multiple_of(EDGE + at, LANES), own)] = total.astype(sum_ref.dtype)
        each_piece(block, lambda copy: copy.start())

    edge = jnp.zeros((rows, EDGE), sum_ref.dtype)
    sum_ref[:, :EDGE] = edge
    sum_ref[:, EDGE + bins:] = edge

    @pl.when(my_bin == 0)
    def _():
        for slot in range(1, bin_size):
            bin_recv[slot, :, :EDGE] = edge

    @pl.when(my_bin == bin_size - 1)
    def _():
        for slot in range(1, bin_size):
            bin_recv[slot, :, EDGE + own:] = edge

    if paired:
        split_multiply(block_at(0), 0, prod_a)
    pl.semaphore_wait(barrier, chan_size + bin_size - 2)

    def one_block(p, _):
        compute(p)
        for offset in range(1, chan_size):
            chan_copy(p, offset).start()

        @pl.when(p > 0)
        def _():
            forward(p - 1)

        return 0

    lax.fori_loop(0, bin_size, one_block, 0)
    forward(bin_size - 1)

    total = sum_ref[:, pl.ds(pl.multiple_of(my_bin * own, LANES), width)].astype(jnp.float32)
    for slot in range(1, bin_size):
        for piece in range(3):
            begin, size = ((EDGE, own), (0, EDGE), (EDGE + own, EDGE))[piece]
            sender = lax.rem(my_bin + slot, bin_size)
            comes = (True, my_bin > 0, my_bin < bin_size - 1)[piece]

            @pl.when(comes)
            def _():
                pltpu.make_async_remote_copy(
                    src_ref=sum_ref.at[:, begin:begin + size],
                    dst_ref=bin_recv.at[slot, :, begin:begin + size],
                    send_sem=bin_sems.at[0, piece, slot],
                    recv_sem=bin_sems.at[1, piece, slot],
                    device_id={"bin": sender},
                    device_id_type=MESH,
                ).wait_recv()

        total += bin_recv[slot].astype(jnp.float32)
    out_ref[...] = (total * scale).astype(jnp.bfloat16).astype(jnp.float32)

    def drain(p, _):
        for offset in range(1, chan_size):
            chan_copy(p, offset).wait_send()
        each_piece(block_at(p), lambda copy: copy.wait_send())
        return 0

    lax.fori_loop(0, bin_size, drain, 0)


def correlate_kernel(trials, signal_ref, bank_ref, ids_ref, out_ref, taps_ref):
    step = pl.program_id(0)
    per_step, templates, bins = out_ref.shape
    bank_size, taps = bank_ref.shape[1:]

    @pl.when(step == 0)
    def _():
        rows = lax.broadcasted_iota(jnp.int32, (bank_size, templates), 0)
        one_hot = (ids_ref[...] == rows).astype(jnp.bfloat16)
        chosen = [
            lax.dot_general(
                one_hot, bank_ref[part], (((0,), (0,)), ((), ())),
                preferred_element_type=jnp.float32,
            )
            for part in (0, 1)
        ]
        taps_ref[:templates, :taps] = chosen[0].astype(jnp.bfloat16)
        taps_ref[:templates, taps:] = (-chosen[1]).astype(jnp.bfloat16)
        taps_ref[templates:, :taps] = chosen[1].astype(jnp.bfloat16)
        taps_ref[templates:, taps:] = chosen[0].astype(jnp.bfloat16)

    row = lax.broadcasted_iota(jnp.int32, (8, LANES), 0)
    col = lax.broadcasted_iota(jnp.int32, (8, LANES), 1)
    spot = (row + col) & (LANES - 1)
    inside = row + col < LANES
    length = bins + taps
    spans = length // LANES
    for t in range(per_step):
        trial = step * per_step + t
        hankel = []
        for part in (0, 1):
            line = signal_ref[pl.ds(part * trials + trial, 1), :]
            turned = [
                take_lanes(jnp.broadcast_to(line[:, s * LANES:(s + 1) * LANES], (8, LANES)), spot)
                for s in range(spans)
            ]
            base = jnp.concatenate(
                [jnp.where(inside, turned[s], turned[(s + 1) % spans]) for s in range(spans)], 1
            )
            rows = [base] + [
                pltpu.roll(base, length - 8 * a, 1) for a in range(1, LANES // 8)
            ]
            hankel.append(jnp.concatenate(rows, 0).astype(jnp.bfloat16))
        wide = jnp.concatenate(
            [
                hankel[part][:, u * LANES:u * LANES + bins]
                for part in (0, 1)
                for u in range(taps // LANES)
            ],
            0,
        )
        response = jnp.dot(taps_ref[...], wide, preferred_element_type=jnp.float32)
        real = response[:templates]
        imag = response[templates:]
        out_ref[t] = (real * real + imag * imag).astype(out_ref.dtype)


def local(spectra, dm_trials, chan_delay, template_bank, template_ids):
    chans, bins = spectra.shape[1:]
    samples = 2 * bins
    bin_size = lax.axis_size("bin")
    chan_size = lax.axis_size("chan")
    trials = dm_trials.shape[0] // chan_size
    templates = template_ids.shape[0]
    taps = template_bank.shape[2]
    own = bins // bin_size
    width = own + 2 * EDGE
    scale = 1.0 / math.sqrt(chan_delay.shape[0])
    per_step = math.gcd(trials, 4)
    if chans % LANES:
        rank = lax.axis_index("chan") * bin_size + lax.axis_index("bin")
        chan_delay = lax.dynamic_slice_in_dim(chan_delay, rank * chans, chans)
    vmem = pl.BlockSpec(memory_space=pltpu.VMEM)
    products = pltpu.VMEM((2 * LANES, 2 * min(bins, 1024)), jnp.float32)

    signal = pl.pallas_call(
        functools.partial(dedisperse_kernel, samples, scale),
        out_shape=jax.ShapeDtypeStruct((2 * trials, width), jnp.float32),
        in_specs=[vmem] * 3,
        out_specs=vmem,
        scratch_shapes=[
            pltpu.VMEM((chan_size, 2 * trials, bins), jnp.bfloat16),
            pltpu.VMEM((2 * trials, bins + 2 * EDGE), jnp.bfloat16),
            pltpu.VMEM((chan_size, 2 * trials, bins), jnp.bfloat16),
            pltpu.VMEM((bin_size, 2 * trials, width), jnp.bfloat16),
            pltpu.VMEM((chans, 2 * bins), jnp.bfloat16),
            pltpu.VMEM((chans, bins), jnp.bfloat16),
            pltpu.VMEM((own, own), jnp.bfloat16),
            pltpu.VMEM((own, own), jnp.bfloat16),
            products,
            products,
            pltpu.SemaphoreType.DMA((2, chan_size, bin_size)),
            pltpu.SemaphoreType.DMA((2, 3, bin_size)),
        ],
        compiler_params=pltpu.CompilerParams(collective_id=0, has_side_effects=True),
        name="dedisperse",
    )(spectra, chan_delay[None, :], dm_trials[None, :])

    return pl.pallas_call(
        functools.partial(correlate_kernel, trials),
        grid=(trials // per_step,),
        out_shape=jax.ShapeDtypeStruct((trials, templates, own), jnp.bfloat16),
        in_specs=[
            pl.BlockSpec((2 * trials, width), lambda t: (0, 0)),
            pl.BlockSpec(template_bank.shape, lambda t: (0, 0, 0)),
            pl.BlockSpec((1, templates), lambda t: (0, 0)),
        ],
        out_specs=pl.BlockSpec((per_step, templates, own), lambda t: (t, 0, 0)),
        scratch_shapes=[pltpu.VMEM((2 * templates, 2 * taps), jnp.bfloat16)],
        name="templates",
    )(signal, template_bank, template_ids[None, :])


def solution(mesh):
    in_specs = (P(None, ("beam", "chan", "bin"), None), P(), P(), P(), P())
    out_specs = P(("beam", "chan"), None, "bin")
    return jax.shard_map(local, mesh=mesh, in_specs=in_specs, out_specs=out_specs, check_vma=False)
```

profile of v0, /device:TPU:0, one launch (start us, length us, event | category | flops | bytes accessed | tf_op | source)
XLA Modules:
  0.0 25.4 jit_solution(12082472900681931409)
XLA Ops:
  0.0 19.9 %dedisperse.1.signal_ref = f32[32,512]{1,0:T(8,128)} custom-call(bf16[2,256,1024]{2,1,0:T(8,128)(2,1)} %spec_ref.1, s32[1,4096]{1,0:T(1,128)} %bitcast.3, s32[1,64]{1,0:T(1,128)} %bitcast.5), custom_call_target="tpu_custom_call" | custom-call | tf_op jit(solution)/shard_map/dedisperse/pallas_call | solution.py:441
  19.9 5.5 %templates.1 = bf16[16,128,256]{2,1,0:T(8,128)(2,1)} custom-call(f32[32,512]{1,0:T(8,128)} %dedisperse.1.signal_ref, bf16[2,256,256]{2,1,0:T(8,128)(2,1)} %bank_ref.1, s32[1,128]{1,0:T(1,128)} %bitcast.4), custom_call_target="tpu_custom_call" | custom-call | tf_op jit(solution)/shard_map/templates/pallas_call | solution.py:464
where the time goes:
time: 25.5 us; the launch traced here: 25.4 us
  Pallas kernels  25.4 us (100%)
    pallas_call x1, Pallas kernels, local(): pl.pallas_call(functools.partial(dedisperse_kernel, samples, scale), out_...  19.9 us
    pallas_call x1, Pallas kernels, local(): pl.pallas_call(functools.partial(correlate_kernel, trials), grid=(trials...  5.46 us

commit v1 on v0

--- a/solution.py
+++ b/solution.py
@@ -353,6 +353,311 @@
 
         total += bin_recv[slot].astype(jnp.float32)
     out_ref[...] = (total * scale).astype(jnp.bfloat16).astype(jnp.float32)
+
+    def drain(p, _):
+        for offset in range(1, chan_size):
+            chan_copy(p, offset).wait_send()
+        each_piece(block_at(p), lambda copy: copy.wait_send())
+        return 0
+
+    lax.fori_loop(0, bin_size, drain, 0)
+
+
+def gather_lanes(x, index):
+    return lax.gather(
+        x, index[:, :, None],
+        dimension_numbers=lax.GatherDimensionNumbers(
+            offset_dims=(), collapsed_slice_dims=(1,), start_index_map=(1,),
+            operand_batching_dims=(0,), start_indices_batching_dims=(0,),
+        ),
+        slice_sizes=(1, 1), mode="promise_in_bounds",
+    )
+
+
+def paired_kernel(
+    samples, scale, spec_hbm, delay_hbm, dm_hbm, out_ref, spec_ref, delay_ref, dm_ref, send_ref,
+    sum_ref, chan_recv, bin_recv, low_ref, table_ref, split_ref, odd_ref, even_ref,
+    load_sems, chan_sems, bin_sems,
+):
+    bin_size = lax.axis_size("bin")
+    chan_size = lax.axis_size("chan")
+    my_bin = lax.axis_index("bin")
+    my_chan = lax.axis_index("chan")
+    chans = spec_ref.shape[1]
+    bins = spec_ref.shape[2]
+    half = samples // 2
+    quarter = half // 2
+    groups, rows = send_ref.shape[:2]
+    width = out_ref.shape[1]
+    tile = LANES
+    own = bins // bin_size
+    count = quarter // LANES
+    pack = 16
+
+    def chan_at(offset):
+        return lax.rem(my_chan + offset, chan_size)
+
+    def bin_at(offset):
+        return lax.rem(my_bin + offset, bin_size)
+
+    def block_at(p):
+        return bin_at(p + 1)
+
+    def spec_copy(p):
+        at = pl.ds(pl.multiple_of(block_at(p) * own, LANES), own)
+        return pltpu.make_async_copy(
+            spec_hbm.at[:, :, at], spec_ref.at[:, :, at], load_sems.at[2 + p]
+        )
+
+    rank = my_chan * bin_size + my_bin
+    mine = pl.ds(pl.multiple_of(rank * chans, LANES), chans)
+    delay_copy = pltpu.make_async_copy(delay_hbm.at[:, mine], delay_ref, load_sems.at[0])
+    dm_copy = pltpu.make_async_copy(dm_hbm, dm_ref, load_sems.at[1])
+    delay_copy.start()
+    dm_copy.start()
+    for p in range(bin_size):
+        spec_copy(p).start()
+
+    barrier = pltpu.get_barrier_semaphore()
+
+    def greet_chan(offset, _):
+        pl.semaphore_signal(
+            barrier, inc=1, device_id={"chan": chan_at(offset)}, device_id_type=MESH
+        )
+        return 0
+
+    def greet_bin(offset, _):
+        pl.semaphore_signal(barrier, inc=1, device_id={"bin": bin_at(offset)}, device_id_type=MESH)
+        return 0
+
+    lax.fori_loop(1, chan_size, greet_chan, 0)
+    lax.fori_loop(1, bin_size, greet_bin, 0)
+
+    near = lax.broadcasted_iota(jnp.int32, (own, own), 0)
+    far = lax.broadcasted_iota(jnp.int32, (own, own), 1)
+    source = jnp.where(near < tile, 2 * near + 1, 2 * (near - tile))
+    split_ref[...] = (far == source).astype(jnp.float32).astype(jnp.bfloat16)
+
+    edge = jnp.zeros((rows, EDGE), sum_ref.dtype)
+    sum_ref[:, :EDGE] = edge
+    sum_ref[:, EDGE + bins:] = edge
+
+    @pl.when(my_bin == 0)
+    def _():
+        for slot in range(1, bin_size):
+            bin_recv[slot, :, :EDGE] = edge
+
+    @pl.when(my_bin == bin_size - 1)
+    def _():
+        for slot in range(1, bin_size):
+            bin_recv[slot, :, EDGE + own:] = edge
+
+    delay_copy.wait()
+    delay = delay_ref[...]
+
+    def rotations(factor):
+        return cos_sin((factor * delay) & (samples - 1), samples)
+
+    row = lax.broadcasted_iota(jnp.int32, (8, chans), 0)
+    fine_cos, fine_sin = rotations(2 * row)
+    mid_cos, mid_sin = rotations(2 * 8 * lax.broadcasted_iota(jnp.int32, (LANES // 8, chans), 0))
+    high_cos, high_sin = rotations(jnp.where(row == 0, 1, 2 * LANES * row))
+    one_cos, one_sin = high_cos[:1], high_sin[:1]
+    for a in range(LANES // 8):
+        at = slice(8 * a, 8 * a + 8)
+        cos = fine_cos * mid_cos[a:a + 1] - fine_sin * mid_sin[a:a + 1]
+        sin = fine_sin * mid_cos[a:a + 1] + fine_cos * mid_sin[a:a + 1]
+        low_ref[0, at] = cos
+        low_ref[1, at] = sin
+        low_ref[2, at] = cos * one_cos - sin * one_sin
+        low_ref[3, at] = sin * one_cos + cos * one_sin
+
+    def fill(i, _):
+        at = pl.ds(pl.multiple_of(i * pack, pack), pack)
+        for odd in (0, 1):
+            low_cos = low_ref[2 * odd, at]
+            low_sin = low_ref[2 * odd + 1, at]
+            for k in range(count):
+                if k == 0:
+                    cos, sin = low_cos, low_sin
+                else:
+                    block_cos, block_sin = high_cos[k:k + 1], high_sin[k:k + 1]
+                    cos = low_cos * block_cos - low_sin * block_sin
+                    sin = low_sin * block_cos + low_cos * block_sin
+                for part, value in ((0, cos), (1, sin)):
+                    first = ((2 * odd + part) * count + k) * LANES
+                    to = pl.ds(pl.multiple_of(first + i * pack, pack), pack)
+                    table_ref[to] = value.astype(jnp.bfloat16)
+        return 0
+
+    lax.fori_loop(0, LANES // pack, fill, 0)
+    parity = (1 - 2 * (delay & 1)).astype(jnp.float32)
+    top = lax.broadcasted_iota(jnp.int32, (pack, chans), 0) == 0
+    table_ref[quarter:quarter + pack] = jnp.where(top, parity, low_ref[1, :pack]).astype(
+        jnp.bfloat16
+    )
+
+    dm_copy.wait()
+    lane = lax.broadcasted_iota(jnp.int32, (8, LANES), 1)
+    dm = jnp.broadcast_to(dm_ref[...], (8, dm_ref.shape[1]))
+    dm = jnp.concatenate([dm] * (LANES // dm_ref.shape[1]), 1)
+    dm = take_lanes(dm, (lane // rows) * (rows // 2) + lane % (rows // 2))
+    dm = jnp.concatenate([dm] * (pack // 8), 0)
+    lane = lax.broadcasted_iota(jnp.int32, (pack, LANES), 1)
+    is_real = (lane // (rows // 2)) % 2 == 0
+    flip = jnp.where(is_real, 1.0, -1.0)
+
+    def turned(block):
+        at = pl.ds(pl.multiple_of(block * own, LANES), own)
+        sides = [
+            lax.dot_general(
+                split_ref[...], spec_ref[part, :, at], (((1,), (1,)), ((), ())),
+                preferred_element_type=jnp.float32,
+            ).astype(jnp.bfloat16)
+            for part in (0, 1)
+        ]
+        return [
+            jnp.concatenate([side[n * tile:(n + 1) * tile] for side in sides], 0) for n in (0, 1)
+        ]
+
+    def multiply(left, prod_ref):
+        size = prod_ref.shape[1]
+        prod_ref[...] = lax.dot_general(
+            left, table_ref[:size], (((1,), (1,)), ((), ())), preferred_element_type=jnp.float32
+        ).astype(jnp.bfloat16)
+
+    def collect(block, even, prod_ref):
+        size = half >> even
+        pieces = []
+        for r in range(tile // pack):
+            spots = r * pack + lax.broadcasted_iota(jnp.int32, (pack, LANES), 0)
+            if even:
+                turns = ((block * tile + spots) * dm) & (2 * size - 1)
+            else:
+                turns = ((block * own + 2 * spots + 1) * dm) & (2 * size - 1)
+            index = jnp.where(turns > size, 2 * size - turns, turns) & (size - 1)
+            if even:
+                which, places = index // LANES, list(range(count))
+            else:
+                which = (index >> 1) // LANES + (index & 1) * (2 * count)
+                places = list(range(count)) + list(range(2 * count, 3 * count))
+                index = index >> 1
+            spot = (index & (LANES - 1)).astype(jnp.int16)
+            which = which.astype(jnp.int16)
+            acc = [None] * 4
+            for b in places:
+                hit = which == b
+                for i, (part, table) in enumerate(((0, 0), (1, 1), (1, 0), (0, 1))):
+                    top = part * tile + r * pack
+                    left = (b + table * count) * LANES
+                    piece = gather_lanes(prod_ref[top:top + pack, left:left + LANES], spot)
+                    acc[i] = piece if acc[i] is None else jnp.where(hit, piece, acc[i])
+            a, b, a2, b2 = [value.astype(jnp.float32) for value in acc]
+            sign = jnp.where(turns > size, -flip, jnp.where(turns == 0, 0.0, flip))
+            sums = jnp.where(is_real, a, a2) + sign * jnp.where(is_real, b, b2)
+            pieces.append(
+                jnp.where(turns == size, jnp.where(is_real, b2, b), sums).astype(jnp.bfloat16)
+            )
+        return pieces
+
+    def compute(p):
+        block = block_at(p)
+        odd, even = turned(block)
+        multiply(odd, odd_ref)
+        multiply(even, even_ref)
+        near = collect(block, 0, odd_ref)
+        far = collect(block, 1, even_ref)
+        part = len(near) // 2
+        for t in (0, 1):
+            picked = near[t * part:(t + 1) * part] + far[t * part:(t + 1) * part]
+            at = pl.ds(pl.multiple_of(block * own + t * tile, LANES), tile)
+            send_ref[:, :, at] = jnp.concatenate(picked, 0).T.reshape(groups, rows, tile)
+
+    def chan_copy(p, offset):
+        at = pl.ds(pl.multiple_of(block_at(p) * own, LANES), own)
+        return pltpu.make_async_remote_copy(
+            src_ref=send_ref.at[chan_at(offset), :, at],
+            dst_ref=chan_recv.at[chan_size - offset, :, at],
+            send_sem=chan_sems.at[0, offset, p],
+            recv_sem=chan_sems.at[1, chan_size - offset, p],
+            device_id={"chan": chan_at(offset)},
+            device_id_type=MESH,
+        )
+
+    def bin_copy(block, piece):
+        to = block + (0, 1, -1)[piece]
+        begin, size, land = ((0, own, EDGE), (own - EDGE, EDGE, 0), (0, EDGE, EDGE + own))[piece]
+        offset = lax.rem(to - my_bin + bin_size, bin_size)
+        slot = lax.rem(bin_size - offset, bin_size)
+        return pltpu.make_async_remote_copy(
+            src_ref=sum_ref.at[:, pl.ds(pl.multiple_of(EDGE + block * own + begin, LANES), size)],
+            dst_ref=bin_recv.at[slot, :, land:land + size],
+            send_sem=bin_sems.at[0, piece, offset],
+            recv_sem=bin_sems.at[1, piece, slot],
+            device_id={"bin": to},
+            device_id_type=MESH,
+        )
+
+    def each_piece(block, act):
+        for piece in range(3):
+            to = block + (0, 1, -1)[piece]
+
+            @pl.when((to >= 0) & (to < bin_size) & (to != my_bin))
+            def _():
+                act(bin_copy(block, piece))
+
+    def forward(p):
+        block = block_at(p)
+        at = pl.multiple_of(block * own, LANES)
+        for offset in range(1, chan_size):
+            chan_copy(p, chan_size - offset).wait_recv()
+        total = send_ref[my_chan, :, pl.ds(at, own)].astype(jnp.float32)
+        for offset in range(1, chan_size):
+            total += chan_recv[offset, :, pl.ds(at, own)].astype(jnp.float32)
+        sum_ref[:, pl.ds(pl.multiple_of(EDGE + at, LANES), own)] = total.astype(sum_ref.dtype)
+        each_piece(block, lambda copy: copy.start())
+
+    def one_block(p, _):
+        spec_copy(p).wait()
+        compute(p)
+
+        @pl.when(p == 0)
+        def _():
+            pl.semaphore_wait(barrier, chan_size + bin_size - 2)
+
+        for offset in range(1, chan_size):
+            chan_copy(p, offset).start()
+        return 0
+
+    lax.fori_loop(0, bin_size, one_block, 0)
+    for p in range(bin_size):
+        forward(p)
+
+    total = sum_ref[:, pl.ds(pl.multiple_of(my_bin * own, LANES), width)].astype(jnp.float32)
+    for slot in range(1, bin_size):
+        for piece in range(3):
+            begin, size = ((EDGE, own), (0, EDGE), (EDGE + own, EDGE))[piece]
+            sender = lax.rem(my_bin + slot, bin_size)
+            comes = (True, my_bin > 0, my_bin < bin_size - 1)[piece]
+
+            @pl.when(comes)
+            def _():
+                pltpu.make_async_remote_copy(
+                    src_ref=sum_ref.at[:, begin:begin + size],
+                    dst_ref=bin_recv.at[slot, :, begin:begin + size],
+                    send_sem=bin_sems.at[0, piece, slot],
+                    recv_sem=bin_sems.at[1, piece, slot],
+                    device_id={"bin": sender},
+                    device_id_type=MESH,
+                ).wait_recv()
+
+        total += bin_recv[slot].astype(jnp.float32)
+    signal = (total * scale).astype(jnp.bfloat16).astype(jnp.float32)
+    lane = lax.broadcasted_iota(jnp.int32, (rows, tile), 1)
+    back = (lane >> 1) + (tile // 2) * (1 - (lane & 1))
+    for t in range(width // tile):
+        at = slice(t * tile, (t + 1) * tile)
+        out_ref[:, at] = take_lanes(signal[:, at], back)
 
     def drain(p, _):
         for offset in range(1, chan_size):
@@ -438,28 +743,65 @@
     vmem = pl.BlockSpec(memory_space=pltpu.VMEM)
     products = pltpu.VMEM((2 * LANES, 2 * min(bins, 1024)), jnp.float32)
 
-    signal = pl.pallas_call(
-        functools.partial(dedisperse_kernel, samples, scale),
-        out_shape=jax.ShapeDtypeStruct((2 * trials, width), jnp.float32),
-        in_specs=[vmem] * 3,
-        out_specs=vmem,
-        scratch_shapes=[
-            pltpu.VMEM((chan_size, 2 * trials, bins), jnp.bfloat16),
-            pltpu.VMEM((2 * trials, bins + 2 * EDGE), jnp.bfloat16),
-            pltpu.VMEM((chan_size, 2 * trials, bins), jnp.bfloat16),
-            pltpu.VMEM((bin_size, 2 * trials, width), jnp.bfloat16),
-            pltpu.VMEM((chans, 2 * bins), jnp.bfloat16),
-            pltpu.VMEM((chans, bins), jnp.bfloat16),
-            pltpu.VMEM((own, own), jnp.bfloat16),
-            pltpu.VMEM((own, own), jnp.bfloat16),
-            products,
-            products,
-            pltpu.SemaphoreType.DMA((2, chan_size, bin_size)),
-            pltpu.SemaphoreType.DMA((2, 3, bin_size)),
-        ],
-        compiler_params=pltpu.CompilerParams(collective_id=0, has_side_effects=True),
-        name="dedisperse",
-    )(spectra, chan_delay[None, :], dm_trials[None, :])
+    paired = (
+        bins <= 1024 and bins % (4 * LANES) == 0 and own == 2 * LANES and chans % LANES == 0
+        and trials * 2 * chan_size == LANES
+    )
+    if paired:
+        hbm = pl.BlockSpec(memory_space=pltpu.HBM)
+        signal = pl.pallas_call(
+            functools.partial(paired_kernel, samples, scale),
+            out_shape=jax.ShapeDtypeStruct((2 * trials, width), jnp.float32),
+            in_specs=[hbm] * 3,
+            out_specs=vmem,
+            scratch_shapes=[
+                pltpu.VMEM((2, chans, bins), jnp.bfloat16),
+                pltpu.VMEM((1, chans), jnp.int32),
+                pltpu.VMEM((1, dm_trials.shape[0]), jnp.int32),
+                pltpu.VMEM((chan_size, 2 * trials, bins), jnp.bfloat16),
+                pltpu.VMEM((2 * trials, bins + 2 * EDGE), jnp.bfloat16),
+                pltpu.VMEM((chan_size, 2 * trials, bins), jnp.bfloat16),
+                pltpu.VMEM((bin_size, 2 * trials, width), jnp.bfloat16),
+                pltpu.VMEM((4, LANES, chans), jnp.float32),
+                pltpu.VMEM((2 * bins, chans), jnp.bfloat16),
+                pltpu.VMEM((own, own), jnp.bfloat16),
+                pltpu.VMEM((2 * LANES, 2 * bins), jnp.bfloat16),
+                pltpu.VMEM((2 * LANES, bins), jnp.bfloat16),
+                pltpu.SemaphoreType.DMA((2 + bin_size,)),
+                pltpu.SemaphoreType.DMA((2, chan_size, bin_size)),
+                pltpu.SemaphoreType.DMA((2, 3, bin_size)),
+            ],
+            compiler_params=pltpu.CompilerParams(
+                collective_id=0, has_side_effects=True, vmem_limit_bytes=24 * 2 ** 20
+            ),
+            name="dedisperse",
+        )(*[
+            pltpu.with_memory_space_constraint(x, pltpu.HBM)
+            for x in (spectra, chan_delay[None, :], dm_trials[None, :])
+        ])
+    else:
+        signal = pl.pallas_call(
+            functools.partial(dedisperse_kernel, samples, scale),
+            out_shape=jax.ShapeDtypeStruct((2 * trials, width), jnp.float32),
+            in_specs=[vmem] * 3,
+            out_specs=vmem,
+            scratch_shapes=[
+                pltpu.VMEM((chan_size, 2 * trials, bins), jnp.bfloat16),
+                pltpu.VMEM((2 * trials, bins + 2 * EDGE), jnp.bfloat16),
+                pltpu.VMEM((chan_size, 2 * trials, bins), jnp.bfloat16),
+                pltpu.VMEM((bin_size, 2 * trials, width), jnp.bfloat16),
+                pltpu.VMEM((chans, 2 * bins), jnp.bfloat16),
+                pltpu.VMEM((chans, bins), jnp.bfloat16),
+                pltpu.VMEM((own, own), jnp.bfloat16),
+                pltpu.VMEM((own, own), jnp.bfloat16),
+                products,
+                products,
+                pltpu.SemaphoreType.DMA((2, chan_size, bin_size)),
+                pltpu.SemaphoreType.DMA((2, 3, bin_size)),
+            ],
+            compiler_params=pltpu.CompilerParams(collective_id=0, has_side_effects=True),
+            name="dedisperse",
+        )(spectra, chan_delay[None, :], dm_trials[None, :])
 
     return pl.pallas_call(
         functools.partial(correlate_kernel, trials),
@@ -472,6 +814,7 @@
         ],
         out_specs=pl.BlockSpec((per_step, templates, own), lambda t: (t, 0, 0)),
         scratch_shapes=[pltpu.VMEM((2 * templates, 2 * taps), jnp.bfloat16)],
+        compiler_params=pltpu.CompilerParams(vmem_limit_bytes=16 * 2 ** 20),
         name="templates",
     )(signal, template_bank, template_ids[None, :])
 

time: 25.5 us -> 19.5 us (0.76)
  Pallas kernels: 25.4 us -> 19.3 us
    pallas_call x1, Pallas kernels: 19.9 us -> 14.8 us  [local(): pl.pallas_call(functools.partial(paired_kernel, samples, scale), out_shap...]
    pallas_call x1, Pallas kernels: 5.46 us -> 4.49 us  [local(): pl.pallas_call(functools.partial(correlate_kernel, trials), grid=(trials...]
where the time goes in v1:
time: 19.5 us; the launch traced here: 19.3 us
  Pallas kernels  19.3 us (99%)
    pallas_call x1, Pallas kernels, local(): pl.pallas_call(functools.partial(paired_kernel, samples, scale), out_shap...  14.8 us
    pallas_call x1, Pallas kernels, local(): pl.pallas_call(functools.partial(correlate_kernel, trials), grid=(trials...  4.49 us

profile of v1, /device:TPU:0, one launch (start us, length us, event | category | flops | bytes accessed | tf_op | source)
XLA Modules:
  0.0 19.3 jit_solution(14769079128626690412)
XLA Ops:
  0.0 0.0 copy-start
  0.0 0.0 copy-start.1
  0.0 14.8 %dedisperse.1.signal_ref = f32[32,512]{1,0:T(8,128)S(1)} custom-call(bf16[2,256,1024]{2,1,0:T(8,128)(2,1)} %spec_hbm.1, s32[1,4096]{1,0:T(1,128)} %bitcast.4, s32[1,64]{1,0:T(1,128)} %bitcast.5), custom_call_target="tpu_custom_call" | custom-call | tf_op jit(solution)/shard_map/dedisperse/pallas_call | solution.py:752
  14.8 0.0 copy-done
  14.8 0.0 copy-done.1
  14.8 4.5 %templates.1 = bf16[16,128,256]{2,1,0:T(8,128)(2,1)} custom-call(f32[32,512]{1,0:T(8,128)S(1)} %dedisperse.1.signal_ref, bf16[2,256,256]{2,1,0:T(8,128)(2,1)S(1)} %copy-done, s32[1,128]{1,0:T(1,128)S(1)} %bitcast.3), custom_call_target="tpu_custom_call" | custom-call | tf_op jit(solution)/shard_map/templates/pallas_call | solution.py:806
Async XLA Ops:
  0.0 14.8 %copy-start = (bf16[2,256,256]{2,1,0:T(8,128)(2,1)S(1)}, bf16[2,256,256]{2,1,0:T(8,128)(2,1)}, u32[]{:S(2)}) copy-start(bf16[2,256,256]{2,1,0:T(8,128)(2,1)} %bank_ref.1) | copy-start | bytes 786436
  0.0 14.8 %copy-start.1 = (s32[128]{0:T(128)S(1)}, s32[128]{0:T(128)}, u32[]{:S(2)}) copy-start(s32[128]{0:T(128)} %param.9) | copy-start | bytes 1540

commit v2 on v1

--- a/solution.py
+++ b/solution.py
@@ -668,61 +668,65 @@
     lax.fori_loop(0, bin_size, drain, 0)
 
 
-def correlate_kernel(trials, signal_ref, bank_ref, ids_ref, out_ref, taps_ref):
-    step = pl.program_id(0)
-    per_step, templates, bins = out_ref.shape
+def correlate_kernel(trials, signal_ref, bank_ref, ids_ref, out_hbm, taps_ref, power_ref, sems):
+    _, templates, bins = power_ref.shape
     bank_size, taps = bank_ref.shape[1:]
-
-    @pl.when(step == 0)
-    def _():
-        rows = lax.broadcasted_iota(jnp.int32, (bank_size, templates), 0)
-        one_hot = (ids_ref[...] == rows).astype(jnp.bfloat16)
-        chosen = [
-            lax.dot_general(
-                one_hot, bank_ref[part], (((0,), (0,)), ((), ())),
-                preferred_element_type=jnp.float32,
+    group = math.gcd(trials, 2)
+
+    rows = lax.broadcasted_iota(jnp.int32, (bank_size, templates), 0)
+    one_hot = (ids_ref[...] == rows).astype(jnp.bfloat16)
+    back = (LANES - 1 - lax.broadcasted_iota(jnp.int32, (16, LANES), 1)).astype(jnp.int16)
+    back = jnp.concatenate([back] * (templates // 16), 0)
+    for part in (0, 1):
+        chosen = lax.dot_general(
+            one_hot, bank_ref[part], (((0,), (0,)), ((), ())), preferred_element_type=jnp.float32
+        ).astype(jnp.bfloat16)
+        for u in range(taps // LANES):
+            at = u * LANES
+            turned = gather_lanes(chosen[:, at:at + LANES], back)
+            taps_ref[part * templates:(part + 1) * templates, at:at + LANES] = turned
+            taps_ref[
+                (1 - part) * templates:(2 - part) * templates, taps + at:taps + at + LANES
+            ] = turned if part == 0 else -turned
+
+    pack = 16
+    length = bins + taps
+
+    def out_copy(g):
+        at = pl.ds(g * group, group)
+        return pltpu.make_async_copy(power_ref.at[at], out_hbm.at[at], sems.at[g])
+
+    def one_group(g, _):
+        for t in range(group):
+            trial = g * group + t
+            hankel = []
+            for part in (0, 1):
+                line = signal_ref[pl.ds(part * trials + trial, 1), :]
+                line = jnp.broadcast_to(line, (pack, length)).astype(jnp.bfloat16)
+                rows = [
+                    pltpu.roll(line, length + pack * a - (LANES - 1), 1, stride=1, stride_axis=0)
+                    for a in range(LANES // pack)
+                ]
+                hankel.append(jnp.concatenate(rows, 0))
+            wide = jnp.concatenate(
+                [
+                    hankel[part][:, u * LANES:u * LANES + bins]
+                    for part in (0, 1)
+                    for u in range(taps // LANES)
+                ],
+                0,
             )
-            for part in (0, 1)
-        ]
-        taps_ref[:templates, :taps] = chosen[0].astype(jnp.bfloat16)
-        taps_ref[:templates, taps:] = (-chosen[1]).astype(jnp.bfloat16)
-        taps_ref[templates:, :taps] = chosen[1].astype(jnp.bfloat16)
-        taps_ref[templates:, taps:] = chosen[0].astype(jnp.bfloat16)
-
-    row = lax.broadcasted_iota(jnp.int32, (8, LANES), 0)
-    col = lax.broadcasted_iota(jnp.int32, (8, LANES), 1)
-    spot = (row + col) & (LANES - 1)
-    inside = row + col < LANES
-    length = bins + taps
-    spans = length // LANES
-    for t in range(per_step):
-        trial = step * per_step + t
-        hankel = []
-        for part in (0, 1):
-            line = signal_ref[pl.ds(part * trials + trial, 1), :]
-            turned = [
-                take_lanes(jnp.broadcast_to(line[:, s * LANES:(s + 1) * LANES], (8, LANES)), spot)
-                for s in range(spans)
-            ]
-            base = jnp.concatenate(
-                [jnp.where(inside, turned[s], turned[(s + 1) % spans]) for s in range(spans)], 1
-            )
-            rows = [base] + [
-                pltpu.roll(base, length - 8 * a, 1) for a in range(1, LANES // 8)
-            ]
-            hankel.append(jnp.concatenate(rows, 0).astype(jnp.bfloat16))
-        wide = jnp.concatenate(
-            [
-                hankel[part][:, u * LANES:u * LANES + bins]
-                for part in (0, 1)
-                for u in range(taps // LANES)
-            ],
-            0,
-        )
-        response = jnp.dot(taps_ref[...], wide, preferred_element_type=jnp.float32)
-        real = response[:templates]
-        imag = response[templates:]
-        out_ref[t] = (real * real + imag * imag).astype(out_ref.dtype)
+            response = jnp.dot(taps_ref[...], wide, preferred_element_type=jnp.float32)
+            real = response[:templates]
+            imag = response[templates:]
+            power_ref[trial] = (real * real + imag * imag).astype(power_ref.dtype)
+        out_copy(g).start()
+        return 0
+
+    for g in range(trials // group):
+        one_group(g, 0)
+    for g in range(trials // group):
+        out_copy(g).wait()
 
 
 def local(spectra, dm_trials, chan_delay, template_bank, template_ids):
@@ -736,7 +740,6 @@
     own = bins // bin_size
     width = own + 2 * EDGE
     scale = 1.0 / math.sqrt(chan_delay.shape[0])
-    per_step = math.gcd(trials, 4)
     if chans % LANES:
         rank = lax.axis_index("chan") * bin_size + lax.axis_index("bin")
         chan_delay = lax.dynamic_slice_in_dim(chan_delay, rank * chans, chans)
@@ -805,15 +808,14 @@
 
     return pl.pallas_call(
         functools.partial(correlate_kernel, trials),
-        grid=(trials // per_step,),
         out_shape=jax.ShapeDtypeStruct((trials, templates, own), jnp.bfloat16),
-        in_specs=[
-            pl.BlockSpec((2 * trials, width), lambda t: (0, 0)),
-            pl.BlockSpec(template_bank.shape, lambda t: (0, 0, 0)),
-            pl.BlockSpec((1, templates), lambda t: (0, 0)),
+        in_specs=[vmem] * 3,
+        out_specs=pl.BlockSpec(memory_space=pltpu.HBM),
+        scratch_shapes=[
+            pltpu.VMEM((2 * templates, 2 * taps), jnp.bfloat16),
+            pltpu.VMEM((trials, templates, own), jnp.bfloat16),
+            pltpu.SemaphoreType.DMA((trials,)),
         ],
-        out_specs=pl.BlockSpec((per_step, templates, own), lambda t: (t, 0, 0)),
-        scratch_shapes=[pltpu.VMEM((2 * templates, 2 * taps), jnp.bfloat16)],
         compiler_params=pltpu.CompilerParams(vmem_limit_bytes=16 * 2 ** 20),
         name="templates",
     )(signal, template_bank, template_ids[None, :])

time: 19.5 us -> 17.3 us (0.89)
  Pallas kernels: 19.3 us -> 17.1 us
    pallas_call x1, Pallas kernels: 4.49 us -> 2.33 us  [local(): pl.pallas_call(functools.partial(correlate_kernel, trials), out_shape=jax...]
where the time goes in v2:
time: 17.3 us; the launch traced here: 17.2 us
  Pallas kernels  17.1 us (99%)
    pallas_call x1, Pallas kernels, local(): pl.pallas_call(functools.partial(paired_kernel, samples, scale), out_shap...  14.8 us
    pallas_call x1, Pallas kernels, local(): pl.pallas_call(functools.partial(correlate_kernel, trials), out_shape=jax...  2.33 us

profile of v2, /device:TPU:0, one launch (start us, length us, event | category | flops | bytes accessed | tf_op | source)
XLA Modules:
  0.0 17.2 jit_solution(7536182086185208530)
XLA Ops:
  0.0 0.0 copy-start
  0.0 0.0 copy-start.1
  0.0 14.8 %dedisperse.1.signal_ref = f32[32,512]{1,0:T(8,128)S(1)} custom-call(bf16[2,256,1024]{2,1,0:T(8,128)(2,1)} %spec_hbm.1, s32[1,4096]{1,0:T(1,128)} %bitcast.4, s32[1,64]{1,0:T(1,128)} %bitcast.5), custom_call_target="tpu_custom_call" | custom-call | tf_op jit(solution)/shard_map/dedisperse/pallas_call | solution.py:755
  14.8 0.0 copy-done
  14.8 0.0 copy-done.1
  14.8 2.3 %templates.1 = bf16[16,128,256]{2,1,0:T(8,128)(2,1)} custom-call(f32[32,512]{1,0:T(8,128)S(1)} %dedisperse.1.signal_ref, bf16[2,256,256]{2,1,0:T(8,128)(2,1)S(1)} %copy-done, s32[1,128]{1,0:T(1,128)S(1)} %bitcast.3), custom_call_target="tpu_custom_call" | custom-call | tf_op jit(solution)/shard_map/templates/pallas_call | solution.py:809
Async XLA Ops:
  0.0 14.8 %copy-start = (bf16[2,256,256]{2,1,0:T(8,128)(2,1)S(1)}, bf16[2,256,256]{2,1,0:T(8,128)(2,1)}, u32[]{:S(2)}) copy-start(bf16[2,256,256]{2,1,0:T(8,128)(2,1)} %bank_ref.1) | copy-start | bytes 786436
  0.0 14.8 %copy-start.1 = (s32[128]{0:T(128)S(1)}, s32[128]{0:T(128)}, u32[]{:S(2)}) copy-start(s32[128]{0:T(128)} %param.9) | copy-start | bytes 1540

commit v3 on v2

--- a/solution.py
+++ b/solution.py
@@ -15,7 +15,7 @@
 
 def cos_sin(turns, samples):
     eighth = samples // 8
-    quadrant = (turns + eighth) // (2 * eighth)
+    quadrant = lax.shift_right_logical(turns + eighth, eighth.bit_length())
     rest = turns - quadrant * (2 * eighth)
     x = rest.astype(jnp.float32) * (2.0 * math.pi / samples)
     y = x * x
@@ -387,15 +387,23 @@
     bins = spec_ref.shape[2]
     half = samples // 2
     quarter = half // 2
-    groups, rows = send_ref.shape[:2]
+    groups, _, rows, _ = send_ref.shape
     width = out_ref.shape[1]
     tile = LANES
     own = bins // bin_size
+    cut = own // tile
+    spans = width // tile
     count = quarter // LANES
     pack = 16
 
+    pairs = chan_size // 2
+    partners = list(range(2, chan_size)) + [1]
+
     def chan_at(offset):
-        return lax.rem(my_chan + offset, chan_size)
+        return (my_chan // 2 + offset // 2) % pairs * 2 + (my_chan + offset) % 2
+
+    def mirror(offset):
+        return (pairs - offset // 2) % pairs * 2 + offset % 2
 
     def bin_at(offset):
         return lax.rem(my_bin + offset, bin_size)
@@ -430,27 +438,29 @@
         pl.semaphore_signal(barrier, inc=1, device_id={"bin": bin_at(offset)}, device_id_type=MESH)
         return 0
 
-    lax.fori_loop(1, chan_size, greet_chan, 0)
-    lax.fori_loop(1, bin_size, greet_bin, 0)
+    for offset in range(1, bin_size):
+        greet_bin(offset, 0)
+    for offset in partners:
+        greet_chan(offset, 0)
 
     near = lax.broadcasted_iota(jnp.int32, (own, own), 0)
     far = lax.broadcasted_iota(jnp.int32, (own, own), 1)
     source = jnp.where(near < tile, 2 * near + 1, 2 * (near - tile))
     split_ref[...] = (far == source).astype(jnp.float32).astype(jnp.bfloat16)
 
-    edge = jnp.zeros((rows, EDGE), sum_ref.dtype)
-    sum_ref[:, :EDGE] = edge
-    sum_ref[:, EDGE + bins:] = edge
+    edge = jnp.zeros((rows, tile), sum_ref.dtype)
+    sum_ref[0] = edge
+    sum_ref[sum_ref.shape[0] - 1] = edge
 
     @pl.when(my_bin == 0)
     def _():
         for slot in range(1, bin_size):
-            bin_recv[slot, :, :EDGE] = edge
+            bin_recv[slot, 0] = edge
 
     @pl.when(my_bin == bin_size - 1)
     def _():
         for slot in range(1, bin_size):
-            bin_recv[slot, :, EDGE + own:] = edge
+            bin_recv[slot, spans - 1] = edge
 
     delay_copy.wait()
     delay = delay_ref[...]
@@ -504,8 +514,9 @@
     dm = take_lanes(dm, (lane // rows) * (rows // 2) + lane % (rows // 2))
     dm = jnp.concatenate([dm] * (pack // 8), 0)
     lane = lax.broadcasted_iota(jnp.int32, (pack, LANES), 1)
-    is_real = (lane // (rows // 2)) % 2 == 0
-    flip = jnp.where(is_real, 1.0, -1.0)
+    real = 1 - (lane // (rows // 2)) % 2
+    is_real = real.astype(jnp.int16) == 1
+    flip = (2 * real - 1).astype(jnp.float32)
 
     def turned(block):
         at = pl.ds(pl.multiple_of(block * own, LANES), own)
@@ -526,24 +537,30 @@
             left, table_ref[:size], (((1,), (1,)), ((), ())), preferred_element_type=jnp.float32
         ).astype(jnp.bfloat16)
 
+    spots = lax.broadcasted_iota(jnp.int32, (pack, LANES), 0)
+    steps = [[(spots * factor + shift) * dm for factor, shift in ((2, 1), (1, 0))],
+             [factor * pack * dm for factor in (2, 1)]]
+    flip = flip.astype(jnp.bfloat16)
+    zero = jnp.zeros((pack, LANES), jnp.bfloat16)
+
     def collect(block, even, prod_ref):
         size = half >> even
+        start = steps[0][even] + (block * (own >> even)) * dm
+        places = list(range(count))
+        if not even:
+            places += list(range(2 * count, 3 * count))
         pieces = []
         for r in range(tile // pack):
-            spots = r * pack + lax.broadcasted_iota(jnp.int32, (pack, LANES), 0)
+            turns = (start + r * steps[1][even]) & (2 * size - 1)
+            index = jnp.minimum(turns, 2 * size - turns) & (size - 1)
             if even:
-                turns = ((block * tile + spots) * dm) & (2 * size - 1)
+                which = index >> 7
             else:
-                turns = ((block * own + 2 * spots + 1) * dm) & (2 * size - 1)
-            index = jnp.where(turns > size, 2 * size - turns, turns) & (size - 1)
-            if even:
-                which, places = index // LANES, list(range(count))
-            else:
-                which = (index >> 1) // LANES + (index & 1) * (2 * count)
-                places = list(range(count)) + list(range(2 * count, 3 * count))
+                which = (index >> 8) + (index & 1) * (2 * count)
                 index = index >> 1
             spot = (index & (LANES - 1)).astype(jnp.int16)
             which = which.astype(jnp.int16)
+            turns = turns.astype(jnp.int16)
             acc = [None] * 4
             for b in places:
                 hit = which == b
@@ -552,12 +569,11 @@
                     left = (b + table * count) * LANES
                     piece = gather_lanes(prod_ref[top:top + pack, left:left + LANES], spot)
                     acc[i] = piece if acc[i] is None else jnp.where(hit, piece, acc[i])
-            a, b, a2, b2 = [value.astype(jnp.float32) for value in acc]
-            sign = jnp.where(turns > size, -flip, jnp.where(turns == 0, 0.0, flip))
-            sums = jnp.where(is_real, a, a2) + sign * jnp.where(is_real, b, b2)
-            pieces.append(
-                jnp.where(turns == size, jnp.where(is_real, b2, b), sums).astype(jnp.bfloat16)
-            )
+            a, b, a2, b2 = acc
+            sign = jnp.where(turns > size, -flip, flip)
+            side = jnp.where(turns == 0, zero, jnp.where(is_real, b, b2) * sign)
+            sums = jnp.where(is_real, a, a2) + side
+            pieces.append(jnp.where(turns == size, jnp.where(is_real, b2, b), sums))
         return pieces
 
     def compute(p):
@@ -570,28 +586,27 @@
         part = len(near) // 2
         for t in (0, 1):
             picked = near[t * part:(t + 1) * part] + far[t * part:(t + 1) * part]
-            at = pl.ds(pl.multiple_of(block * own + t * tile, LANES), tile)
-            send_ref[:, :, at] = jnp.concatenate(picked, 0).T.reshape(groups, rows, tile)
+            send_ref[:, block * cut + t] = jnp.concatenate(picked, 0).T.reshape(groups, rows, tile)
 
     def chan_copy(p, offset):
-        at = pl.ds(pl.multiple_of(block_at(p) * own, LANES), own)
+        at = pl.ds(block_at(p) * cut, cut)
         return pltpu.make_async_remote_copy(
-            src_ref=send_ref.at[chan_at(offset), :, at],
-            dst_ref=chan_recv.at[chan_size - offset, :, at],
+            src_ref=send_ref.at[chan_at(offset), at],
+            dst_ref=chan_recv.at[mirror(offset), at],
             send_sem=chan_sems.at[0, offset, p],
-            recv_sem=chan_sems.at[1, chan_size - offset, p],
+            recv_sem=chan_sems.at[1, mirror(offset), p],
             device_id={"chan": chan_at(offset)},
             device_id_type=MESH,
         )
 
     def bin_copy(block, piece):
         to = block + (0, 1, -1)[piece]
-        begin, size, land = ((0, own, EDGE), (own - EDGE, EDGE, 0), (0, EDGE, EDGE + own))[piece]
+        begin, size, land = ((0, cut, 1), (cut - 1, 1, 0), (0, 1, spans - 1))[piece]
         offset = lax.rem(to - my_bin + bin_size, bin_size)
         slot = lax.rem(bin_size - offset, bin_size)
         return pltpu.make_async_remote_copy(
-            src_ref=sum_ref.at[:, pl.ds(pl.multiple_of(EDGE + block * own + begin, LANES), size)],
-            dst_ref=bin_recv.at[slot, :, land:land + size],
+            src_ref=sum_ref.at[pl.ds(1 + block * cut + begin, size)],
+            dst_ref=bin_recv.at[slot, land:land + size],
             send_sem=bin_sems.at[0, piece, offset],
             recv_sem=bin_sems.at[1, piece, slot],
             device_id={"bin": to},
@@ -608,13 +623,13 @@
 
     def forward(p):
         block = block_at(p)
-        at = pl.multiple_of(block * own, LANES)
+        at = pl.ds(block * cut, cut)
         for offset in range(1, chan_size):
-            chan_copy(p, chan_size - offset).wait_recv()
-        total = send_ref[my_chan, :, pl.ds(at, own)].astype(jnp.float32)
+            chan_copy(p, mirror(offset)).wait_recv()
+        total = send_ref[my_chan, at].astype(jnp.float32)
         for offset in range(1, chan_size):
-            total += chan_recv[offset, :, pl.ds(at, own)].astype(jnp.float32)
-        sum_ref[:, pl.ds(pl.multiple_of(EDGE + at, LANES), own)] = total.astype(sum_ref.dtype)
+            total += chan_recv[offset, at].astype(jnp.float32)
+        sum_ref[pl.ds(1 + block * cut, cut)] = total.astype(sum_ref.dtype)
         each_piece(block, lambda copy: copy.start())
 
     def one_block(p, _):
@@ -625,7 +640,7 @@
         def _():
             pl.semaphore_wait(barrier, chan_size + bin_size - 2)
 
-        for offset in range(1, chan_size):
+        for offset in partners:
             chan_copy(p, offset).start()
         return 0
 
@@ -633,18 +648,18 @@
     for p in range(bin_size):
         forward(p)
 
-    total = sum_ref[:, pl.ds(pl.multiple_of(my_bin * own, LANES), width)].astype(jnp.float32)
+    total = sum_ref[pl.ds(my_bin * cut, spans)].astype(jnp.float32)
     for slot in range(1, bin_size):
         for piece in range(3):
-            begin, size = ((EDGE, own), (0, EDGE), (EDGE + own, EDGE))[piece]
+            begin, size = ((1, cut), (0, 1), (spans - 1, 1))[piece]
             sender = lax.rem(my_bin + slot, bin_size)
             comes = (True, my_bin > 0, my_bin < bin_size - 1)[piece]
 
             @pl.when(comes)
             def _():
                 pltpu.make_async_remote_copy(
-                    src_ref=sum_ref.at[:, begin:begin + size],
-                    dst_ref=bin_recv.at[slot, :, begin:begin + size],
+                    src_ref=sum_ref.at[begin:begin + size],
+                    dst_ref=bin_recv.at[slot, begin:begin + size],
                     send_sem=bin_sems.at[0, piece, slot],
                     recv_sem=bin_sems.at[1, piece, slot],
                     device_id={"bin": sender},
@@ -655,9 +670,8 @@
     signal = (total * scale).astype(jnp.bfloat16).astype(jnp.float32)
     lane = lax.broadcasted_iota(jnp.int32, (rows, tile), 1)
     back = (lane >> 1) + (tile // 2) * (1 - (lane & 1))
-    for t in range(width // tile):
-        at = slice(t * tile, (t + 1) * tile)
-        out_ref[:, at] = take_lanes(signal[:, at], back)
+    for t in range(spans):
+        out_ref[:, t * tile:(t + 1) * tile] = take_lanes(signal[t], back)
 
     def drain(p, _):
         for offset in range(1, chan_size):
@@ -748,7 +762,7 @@
 
     paired = (
         bins <= 1024 and bins % (4 * LANES) == 0 and own == 2 * LANES and chans % LANES == 0
-        and trials * 2 * chan_size == LANES
+        and trials * 2 * chan_size == LANES and chan_size % 2 == 0
     )
     if paired:
         hbm = pl.BlockSpec(memory_space=pltpu.HBM)
@@ -761,10 +775,10 @@
                 pltpu.VMEM((2, chans, bins), jnp.bfloat16),
                 pltpu.VMEM((1, chans), jnp.int32),
                 pltpu.VMEM((1, dm_trials.shape[0]), jnp.int32),
-                pltpu.VMEM((chan_size, 2 * trials, bins), jnp.bfloat16),
-                pltpu.VMEM((2 * trials, bins + 2 * EDGE), jnp.bfloat16),
-                pltpu.VMEM((chan_size, 2 * trials, bins), jnp.bfloat16),
-                pltpu.VMEM((bin_size, 2 * trials, width), jnp.bfloat16),
+                pltpu.VMEM((chan_size, bins // LANES, 2 * trials, LANES), jnp.bfloat16),
+                pltpu.VMEM((bins // LANES + 2, 2 * trials, LANES), jnp.bfloat16),
+                pltpu.VMEM((chan_size, bins // LANES, 2 * trials, LANES), jnp.bfloat16),
+                pltpu.VMEM((bin_size, width // LANES, 2 * trials, LANES), jnp.bfloat16),
                 pltpu.VMEM((4, LANES, chans), jnp.float32),
                 pltpu.VMEM((2 * bins, chans), jnp.bfloat16),
                 pltpu.VMEM((own, own), jnp.bfloat16),

time: 17.3 us -> 17.1 us (0.988)
  Pallas kernels: 17.1 us -> 16.9 us
    pallas_call x1, Pallas kernels: 14.8 us -> 14.6 us  [local(): pl.pallas_call(functools.partial(paired_kernel, samples, scale), out_shap...]
where the time goes in v3:
time: 17.1 us; the launch traced here: 16.9 us
  Pallas kernels  16.9 us (99%)
    pallas_call x1, Pallas kernels, local(): pl.pallas_call(functools.partial(paired_kernel, samples, scale), out_shap...  14.6 us
    pallas_call x1, Pallas kernels, local(): pl.pallas_call(functools.partial(correlate_kernel, trials), out_shape=jax...  2.33 us

profile of v3, /device:TPU:0, one launch (start us, length us, event | category | flops | bytes accessed | tf_op | source)
XLA Modules:
  0.0 16.9 jit_solution(8604213052168529219)
XLA Ops:
  0.0 0.0 copy-start
  0.0 0.0 copy-start.1
  0.0 14.6 %dedisperse.1.signal_ref = f32[32,512]{1,0:T(8,128)S(1)} custom-call(bf16[2,256,1024]{2,1,0:T(8,128)(2,1)} %spec_hbm.1, s32[1,4096]{1,0:T(1,128)} %bitcast.4, s32[1,64]{1,0:T(1,128)} %bitcast.5), custom_call_target="tpu_custom_call" | custom-call | tf_op jit(solution)/shard_map/dedisperse/pallas_call | solution.py:769
  14.6 0.0 copy-done
  14.6 0.0 copy-done.1
  14.6 2.3 %templates.1 = bf16[16,128,256]{2,1,0:T(8,128)(2,1)} custom-call(f32[32,512]{1,0:T(8,128)S(1)} %dedisperse.1.signal_ref, bf16[2,256,256]{2,1,0:T(8,128)(2,1)S(1)} %copy-done, s32[1,128]{1,0:T(1,128)S(1)} %bitcast.3), custom_call_target="tpu_custom_call" | custom-call | tf_op jit(solution)/shard_map/templates/pallas_call | solution.py:823
Async XLA Ops:
  0.0 14.6 %copy-start = (bf16[2,256,256]{2,1,0:T(8,128)(2,1)S(1)}, bf16[2,256,256]{2,1,0:T(8,128)(2,1)}, u32[]{:S(2)}) copy-start(bf16[2,256,256]{2,1,0:T(8,128)(2,1)} %bank_ref.1) | copy-start | bytes 786436
  0.0 14.6 %copy-start.1 = (s32[128]{0:T(128)S(1)}, s32[128]{0:T(128)}, u32[]{:S(2)}) copy-start(s32[128]{0:T(128)} %param.9) | copy-start | bytes 1540

commit v4 on v3

--- a/solution.py
+++ b/solution.py
@@ -374,8 +374,29 @@
     )
 
 
+def build_taps(bank_ref, ids_ref, taps_ref):
+    bank_size, taps = bank_ref.shape[1:]
+    templates = ids_ref.shape[1]
+    rows = lax.broadcasted_iota(jnp.int32, (bank_size, templates), 0)
+    one_hot = (ids_ref[...] == rows).astype(jnp.bfloat16)
+    back = (LANES - 1 - lax.broadcasted_iota(jnp.int32, (16, LANES), 1)).astype(jnp.int16)
+    back = jnp.concatenate([back] * (templates // 16), 0)
+    for part in (0, 1):
+        chosen = lax.dot_general(
+            one_hot, bank_ref[part], (((0,), (0,)), ((), ())), preferred_element_type=jnp.float32
+        ).astype(jnp.bfloat16)
+        for u in range(taps // LANES):
+            at = u * LANES
+            turned = gather_lanes(chosen[:, at:at + LANES], back)
+            taps_ref[part * templates:(part + 1) * templates, at:at + LANES] = turned
+            taps_ref[
+                (1 - part) * templates:(2 - part) * templates, taps + at:taps + at + LANES
+            ] = turned if part == 0 else -turned
+
+
 def paired_kernel(
-    samples, scale, spec_hbm, delay_hbm, dm_hbm, out_ref, spec_ref, delay_ref, dm_ref, send_ref,
+    samples, scale, spec_hbm, delay_hbm, dm_hbm, bank_hbm, ids_hbm, out_ref, taps_ref, spec_ref,
+    delay_ref, dm_ref, bank_ref, ids_ref, send_ref,
     sum_ref, chan_recv, bin_recv, low_ref, table_ref, split_ref, odd_ref, even_ref,
     load_sems, chan_sems, bin_sems,
 ):
@@ -425,6 +446,10 @@
     dm_copy.start()
     for p in range(bin_size):
         spec_copy(p).start()
+    bank_copy = pltpu.make_async_copy(bank_hbm, bank_ref, load_sems.at[2 + bin_size])
+    ids_copy = pltpu.make_async_copy(ids_hbm, ids_ref, load_sems.at[3 + bin_size])
+    bank_copy.start()
+    ids_copy.start()
 
     barrier = pltpu.get_barrier_semaphore()
 
@@ -645,6 +670,9 @@
         return 0
 
     lax.fori_loop(0, bin_size, one_block, 0)
+    bank_copy.wait()
+    ids_copy.wait()
+    build_taps(bank_ref, ids_ref, taps_ref)
     for p in range(bin_size):
         forward(p)
 
@@ -682,26 +710,10 @@
     lax.fori_loop(0, bin_size, drain, 0)
 
 
-def correlate_kernel(trials, signal_ref, bank_ref, ids_ref, out_hbm, taps_ref, power_ref, sems):
+def correlate_kernel(trials, signal_ref, taps_ref, out_hbm, power_ref, sems):
     _, templates, bins = power_ref.shape
-    bank_size, taps = bank_ref.shape[1:]
+    taps = taps_ref.shape[1] // 2
     group = math.gcd(trials, 2)
-
-    rows = lax.broadcasted_iota(jnp.int32, (bank_size, templates), 0)
-    one_hot = (ids_ref[...] == rows).astype(jnp.bfloat16)
-    back = (LANES - 1 - lax.broadcasted_iota(jnp.int32, (16, LANES), 1)).astype(jnp.int16)
-    back = jnp.concatenate([back] * (templates // 16), 0)
-    for part in (0, 1):
-        chosen = lax.dot_general(
-            one_hot, bank_ref[part], (((0,), (0,)), ((), ())), preferred_element_type=jnp.float32
-        ).astype(jnp.bfloat16)
-        for u in range(taps // LANES):
-            at = u * LANES
-            turned = gather_lanes(chosen[:, at:at + LANES], back)
-            taps_ref[part * templates:(part + 1) * templates, at:at + LANES] = turned
-            taps_ref[
-                (1 - part) * templates:(2 - part) * templates, taps + at:taps + at + LANES
-            ] = turned if part == 0 else -turned
 
     pack = 16
     length = bins + taps
@@ -766,15 +778,20 @@
     )
     if paired:
         hbm = pl.BlockSpec(memory_space=pltpu.HBM)
-        signal = pl.pallas_call(
+        signal, chosen = pl.pallas_call(
             functools.partial(paired_kernel, samples, scale),
-            out_shape=jax.ShapeDtypeStruct((2 * trials, width), jnp.float32),
-            in_specs=[hbm] * 3,
-            out_specs=vmem,
+            out_shape=[
+                jax.ShapeDtypeStruct((2 * trials, width), jnp.float32),
+                jax.ShapeDtypeStruct((2 * templates, 2 * taps), jnp.bfloat16),
+            ],
+            in_specs=[hbm] * 5,
+            out_specs=[vmem] * 2,
             scratch_shapes=[
                 pltpu.VMEM((2, chans, bins), jnp.bfloat16),
                 pltpu.VMEM((1, chans), jnp.int32),
                 pltpu.VMEM((1, dm_trials.shape[0]), jnp.int32),
+                pltpu.VMEM(template_bank.shape, jnp.bfloat16),
+                pltpu.VMEM((1, templates), jnp.int32),
                 pltpu.VMEM((chan_size, bins // LANES, 2 * trials, LANES), jnp.bfloat16),
                 pltpu.VMEM((bins // LANES + 2, 2 * trials, LANES), jnp.bfloat16),
                 pltpu.VMEM((chan_size, bins // LANES, 2 * trials, LANES), jnp.bfloat16),
@@ -784,7 +801,7 @@
                 pltpu.VMEM((own, own), jnp.bfloat16),
                 pltpu.VMEM((2 * LANES, 2 * bins), jnp.bfloat16),
                 pltpu.VMEM((2 * LANES, bins), jnp.bfloat16),
-                pltpu.SemaphoreType.DMA((2 + bin_size,)),
+                pltpu.SemaphoreType.DMA((4 + bin_size,)),
                 pltpu.SemaphoreType.DMA((2, chan_size, bin_size)),
                 pltpu.SemaphoreType.DMA((2, 3, bin_size)),
             ],
@@ -794,7 +811,10 @@
             name="dedisperse",
         )(*[
             pltpu.with_memory_space_constraint(x, pltpu.HBM)
-            for x in (spectra, chan_delay[None, :], dm_trials[None, :])
+            for x in (
+                spectra, chan_delay[None, :], dm_trials[None, :], template_bank,
+                template_ids[None, :],
+            )
         ])
     else:
         signal = pl.pallas_call(
@@ -820,19 +840,26 @@
             name="dedisperse",
         )(spectra, chan_delay[None, :], dm_trials[None, :])
 
+        chosen = pl.pallas_call(
+            build_taps,
+            out_shape=jax.ShapeDtypeStruct((2 * templates, 2 * taps), jnp.bfloat16),
+            in_specs=[vmem] * 2,
+            out_specs=vmem,
+            name="taps",
+        )(template_bank, template_ids[None, :])
+
     return pl.pallas_call(
         functools.partial(correlate_kernel, trials),
         out_shape=jax.ShapeDtypeStruct((trials, templates, own), jnp.bfloat16),
-        in_specs=[vmem] * 3,
+        in_specs=[vmem] * 2,
         out_specs=pl.BlockSpec(memory_space=pltpu.HBM),
         scratch_shapes=[
-            pltpu.VMEM((2 * templates, 2 * taps), jnp.bfloat16),
             pltpu.VMEM((trials, templates, own), jnp.bfloat16),
             pltpu.SemaphoreType.DMA((trials,)),
         ],
         compiler_params=pltpu.CompilerParams(vmem_limit_bytes=16 * 2 ** 20),
         name="templates",
-    )(signal, template_bank, template_ids[None, :])
+    )(signal, chosen)
 
 
 def solution(mesh):

time: 17.1 us -> 16.9 us (0.988)
  no operation moved by 1% of the time
where the time goes in v4:
time: 16.9 us; the launch traced here: 16.8 us
  Pallas kernels  16.8 us (99%)
    pallas_call x1, Pallas kernels, local(): pl.pallas_call(functools.partial(paired_kernel, samples, scale), out_shap...  14.6 us
    pallas_call x1, Pallas kernels, local(): pl.pallas_call(functools.partial(correlate_kernel, trials), out_shape=jax...  2.19 us

profile of v4, /device:TPU:0, one launch (start us, length us, event | category | flops | bytes accessed | tf_op | source)
XLA Modules:
  0.0 16.8 jit_solution(10115423275689838229)
XLA Ops:
  0.0 14.6 %dedisperse.1 = (f32[32,512]{1,0:T(8,128)S(1)}, bf16[256,512]{1,0:T(8,128)(2,1)S(1)}) custom-call(bf16[2,256,1024]{2,1,0:T(8,128)(2,1)} %spec_hbm.1, s32[1,4096]{1,0:T(1,128)} %bitcast.3, s32[1,64]{1,0:T(1,128)} %bitcast.4, bf16[2,256,256]{2,1,0:T(8,128)(2,1)} %bank_hbm.1, s32[1,128]{1,0:T(1,128)} %bitcast.5), custom_call_target="tpu_custom_call" | custom-call | tf_op jit(solution)/shard_map/dedisperse/pallas_call | solution.py:781
  14.6 2.2 %templates.1 = bf16[16,128,256]{2,1,0:T(8,128)(2,1)} custom-call(f32[32,512]{1,0:T(8,128)S(1)} %get-tuple-element.7.signal_ref, bf16[256,512]{1,0:T(8,128)(2,1)S(1)} %get-tuple-element.8.taps_ref), custom_call_target="tpu_custom_call" | custom-call | tf_op jit(solution)/shard_map/templates/pallas_call | solution.py:851

commit v5 on v4

--- a/solution.py
+++ b/solution.py
@@ -444,29 +444,29 @@
     dm_copy = pltpu.make_async_copy(dm_hbm, dm_ref, load_sems.at[1])
     delay_copy.start()
     dm_copy.start()
+
+    barrier = pltpu.get_barrier_semaphore()
+
+    def greet_chan(offset, _):
+        pl.semaphore_signal(
+            barrier, inc=1, device_id={"chan": chan_at(offset)}, device_id_type=MESH
+        )
+        return 0
+
+    def greet_bin(offset, _):
+        pl.semaphore_signal(barrier, inc=1, device_id={"bin": bin_at(offset)}, device_id_type=MESH)
+        return 0
+
+    for offset in range(1, bin_size):
+        greet_bin(offset, 0)
+    for offset in partners:
+        greet_chan(offset, 0)
     for p in range(bin_size):
         spec_copy(p).start()
     bank_copy = pltpu.make_async_copy(bank_hbm, bank_ref, load_sems.at[2 + bin_size])
     ids_copy = pltpu.make_async_copy(ids_hbm, ids_ref, load_sems.at[3 + bin_size])
     bank_copy.start()
     ids_copy.start()
-
-    barrier = pltpu.get_barrier_semaphore()
-
-    def greet_chan(offset, _):
-        pl.semaphore_signal(
-            barrier, inc=1, device_id={"chan": chan_at(offset)}, device_id_type=MESH
-        )
-        return 0
-
-    def greet_bin(offset, _):
-        pl.semaphore_signal(barrier, inc=1, device_id={"bin": bin_at(offset)}, device_id_type=MESH)
-        return 0
-
-    for offset in range(1, bin_size):
-        greet_bin(offset, 0)
-    for offset in partners:
-        greet_chan(offset, 0)
 
     near = lax.broadcasted_iota(jnp.int32, (own, own), 0)
     far = lax.broadcasted_iota(jnp.int32, (own, own), 1)
@@ -670,11 +670,24 @@
         return 0
 
     lax.fori_loop(0, bin_size, one_block, 0)
+    for p in range(bin_size - 1):
+        forward(p)
     bank_copy.wait()
     ids_copy.wait()
     build_taps(bank_ref, ids_ref, taps_ref)
-    for p in range(bin_size):
-        forward(p)
+    forward(bin_size - 1)
+
+    def drain(p, _):
+        for offset in range(1, chan_size):
+            chan_copy(p, offset).wait_send()
+
+        @pl.when(p + 1 < bin_size)
+        def _():
+            each_piece(block_at(p), lambda copy: copy.wait_send())
+
+        return 0
+
+    lax.fori_loop(0, bin_size, drain, 0)
 
     total = sum_ref[pl.ds(my_bin * cut, spans)].astype(jnp.float32)
     for slot in range(1, bin_size):
@@ -701,13 +714,7 @@
     for t in range(spans):
         out_ref[:, t * tile:(t + 1) * tile] = take_lanes(signal[t], back)
 
-    def drain(p, _):
-        for offset in range(1, chan_size):
-            chan_copy(p, offset).wait_send()
-        each_piece(block_at(p), lambda copy: copy.wait_send())
-        return 0
-
-    lax.fori_loop(0, bin_size, drain, 0)
+    each_piece(block_at(bin_size - 1), lambda copy: copy.wait_send())
 
 
 def correlate_kernel(trials, signal_ref, taps_ref, out_hbm, power_ref, sems):

time: 16.9 us -> 16.8 us (level)
  no operation moved by 1% of the time
where the time goes in v5:
time: 16.8 us; the launch traced here: 16.7 us
  Pallas kernels  16.7 us (99%)
    pallas_call x1, Pallas kernels, local(): pl.pallas_call(functools.partial(paired_kernel, samples, scale), out_shap...  14.5 us
    pallas_call x1, Pallas kernels, local(): pl.pallas_call(functools.partial(correlate_kernel, trials), out_shape=jax...  2.18 us

profile of v5, /device:TPU:0, one launch (start us, length us, event | category | flops | bytes accessed | tf_op | source)
XLA Modules:
  0.0 16.7 jit_solution(8862953410575436056)
XLA Ops:
  0.0 14.5 %dedisperse.1 = (f32[32,512]{1,0:T(8,128)S(1)}, bf16[256,512]{1,0:T(8,128)(2,1)S(1)}) custom-call(bf16[2,256,1024]{2,1,0:T(8,128)(2,1)} %spec_hbm.1, s32[1,4096]{1,0:T(1,128)} %bitcast.3, s32[1,64]{1,0:T(1,128)} %bitcast.4, bf16[2,256,256]{2,1,0:T(8,128)(2,1)} %bank_hbm.1, s32[1,128]{1,0:T(1,128)} %bitcast.5), custom_call_target="tpu_custom_call" | custom-call | tf_op jit(solution)/shard_map/dedisperse/pallas_call | solution.py:788
  14.5 2.2 %templates.1 = bf16[16,128,256]{2,1,0:T(8,128)(2,1)} custom-call(f32[32,512]{1,0:T(8,128)S(1)} %get-tuple-element.7.signal_ref, bf16[256,512]{1,0:T(8,128)(2,1)S(1)} %get-tuple-element.8.taps_ref), custom_call_target="tpu_custom_call" | custom-call | tf_op jit(solution)/shard_map/templates/pallas_call | solution.py:858

commit v6 on v5

--- a/solution.py
+++ b/solution.py
@@ -639,7 +639,7 @@
         )
 
     def each_piece(block, act):
-        for piece in range(3):
+        for piece in (2, 1, 0):
             to = block + (0, 1, -1)[piece]
 
             @pl.when((to >= 0) & (to < bin_size) & (to != my_bin))
@@ -689,24 +689,30 @@
 
     lax.fori_loop(0, bin_size, drain, 0)
 
+    def arrive(piece):
+        begin, size = ((1, cut), (0, 1), (spans - 1, 1))[piece]
+        for slot in range(1, bin_size):
+            pltpu.make_async_remote_copy(
+                src_ref=sum_ref.at[begin:begin + size],
+                dst_ref=bin_recv.at[slot, begin:begin + size],
+                send_sem=bin_sems.at[0, piece, slot],
+                recv_sem=bin_sems.at[1, piece, slot],
+                device_id={"bin": lax.rem(my_bin + slot, bin_size)},
+                device_id_type=MESH,
+            ).wait_recv()
+
+    arrive(0)
+
+    @pl.when(my_bin > 0)
+    def _():
+        arrive(1)
+
+    @pl.when(my_bin < bin_size - 1)
+    def _():
+        arrive(2)
+
     total = sum_ref[pl.ds(my_bin * cut, spans)].astype(jnp.float32)
     for slot in range(1, bin_size):
-        for piece in range(3):
-            begin, size = ((1, cut), (0, 1), (spans - 1, 1))[piece]
-            sender = lax.rem(my_bin + slot, bin_size)
-            comes = (True, my_bin > 0, my_bin < bin_size - 1)[piece]
-
-            @pl.when(comes)
-            def _():
-                pltpu.make_async_remote_copy(
-                    src_ref=sum_ref.at[begin:begin + size],
-                    dst_ref=bin_recv.at[slot, begin:begin + size],
-                    send_sem=bin_sems.at[0, piece, slot],
-                    recv_sem=bin_sems.at[1, piece, slot],
-                    device_id={"bin": sender},
-                    device_id_type=MESH,
-                ).wait_recv()
-
         total += bin_recv[slot].astype(jnp.float32)
     signal = (total * scale).astype(jnp.bfloat16).astype(jnp.float32)
     lane = lax.broadcasted_iota(jnp.int32, (rows, tile), 1)

time: 16.8 us -> 16.7 us (level)
  Pallas kernels: 16.7 us -> 16.5 us
where the time goes in v6:
time: 16.7 us; the launch traced here: 16.6 us
  Pallas kernels  16.5 us (99%)
    pallas_call x1, Pallas kernels, local(): pl.pallas_call(functools.partial(paired_kernel, samples, scale), out_shap...  14.4 us
    pallas_call x1, Pallas kernels, local(): pl.pallas_call(functools.partial(correlate_kernel, trials), out_shape=jax...  2.19 us

profile of v6, /device:TPU:0, one launch (start us, length us, event | category | flops | bytes accessed | tf_op | source)
XLA Modules:
  0.0 16.6 jit_solution(16039783373481345629)
XLA Ops:
  0.0 14.4 %dedisperse.1 = (f32[32,512]{1,0:T(8,128)S(1)}, bf16[256,512]{1,0:T(8,128)(2,1)S(1)}) custom-call(bf16[2,256,1024]{2,1,0:T(8,128)(2,1)} %spec_hbm.1, s32[1,4096]{1,0:T(1,128)} %bitcast.3, s32[1,64]{1,0:T(1,128)} %bitcast.4, bf16[2,256,256]{2,1,0:T(8,128)(2,1)} %bank_hbm.1, s32[1,128]{1,0:T(1,128)} %bitcast.5), custom_call_target="tpu_custom_call" | custom-call | tf_op jit(solution)/shard_map/dedisperse/pallas_call | solution.py:794
  14.4 2.2 %templates.1 = bf16[16,128,256]{2,1,0:T(8,128)(2,1)} custom-call(f32[32,512]{1,0:T(8,128)S(1)} %get-tuple-element.7.signal_ref, bf16[256,512]{1,0:T(8,128)(2,1)S(1)} %get-tuple-element.8.taps_ref), custom_call_target="tpu_custom_call" | custom-call | tf_op jit(solution)/shard_map/templates/pallas_call | solution.py:864

commit v7 on v6

--- a/solution.py
+++ b/solution.py
@@ -701,7 +701,19 @@
                 device_id_type=MESH,
             ).wait_recv()
 
+    lane = lax.broadcasted_iota(jnp.int32, (rows, tile), 1)
+    back = (lane >> 1) + (tile // 2) * (1 - (lane & 1))
+
+    def finish(t):
+        total = sum_ref[my_bin * cut + t].astype(jnp.float32)
+        for slot in range(1, bin_size):
+            total += bin_recv[slot, t].astype(jnp.float32)
+        signal = (total * scale).astype(jnp.bfloat16).astype(jnp.float32)
+        out_ref[:, t * tile:(t + 1) * tile] = take_lanes(signal, back)
+
     arrive(0)
+    for t in range(1, spans - 1):
+        finish(t)
 
     @pl.when(my_bin > 0)
     def _():
@@ -711,15 +723,8 @@
     def _():
         arrive(2)
 
-    total = sum_ref[pl.ds(my_bin * cut, spans)].astype(jnp.float32)
-    for slot in range(1, bin_size):
-        total += bin_recv[slot].astype(jnp.float32)
-    signal = (total * scale).astype(jnp.bfloat16).astype(jnp.float32)
-    lane = lax.broadcasted_iota(jnp.int32, (rows, tile), 1)
-    back = (lane >> 1) + (tile // 2) * (1 - (lane & 1))
-    for t in range(spans):
-        out_ref[:, t * tile:(t + 1) * tile] = take_lanes(signal[t], back)
-
+    finish(0)
+    finish(spans - 1)
     each_piece(block_at(bin_size - 1), lambda copy: copy.wait_send())
 
 

time: 16.7 us -> 16.7 us (level)
  no operation moved by 1% of the time
where the time goes in v7:
time: 16.7 us; the launch traced here: 16.5 us
  Pallas kernels  16.5 us (99%)
    pallas_call x1, Pallas kernels, local(): pl.pallas_call(functools.partial(paired_kernel, samples, scale), out_shap...  14.3 us
    pallas_call x1, Pallas kernels, local(): pl.pallas_call(functools.partial(correlate_kernel, trials), out_shape=jax...  2.18 us

profile of v7, /device:TPU:0, one launch (start us, length us, event | category | flops | bytes accessed | tf_op | source)
XLA Modules:
  0.0 16.5 jit_solution(6493612250480411306)
XLA Ops:
  0.0 14.3 %dedisperse.1 = (f32[32,512]{1,0:T(8,128)S(1)}, bf16[256,512]{1,0:T(8,128)(2,1)S(1)}) custom-call(bf16[2,256,1024]{2,1,0:T(8,128)(2,1)} %spec_hbm.1, s32[1,4096]{1,0:T(1,128)} %bitcast.3, s32[1,64]{1,0:T(1,128)} %bitcast.4, bf16[2,256,256]{2,1,0:T(8,128)(2,1)} %bank_hbm.1, s32[1,128]{1,0:T(1,128)} %bitcast.5), custom_call_target="tpu_custom_call" | custom-call | tf_op jit(solution)/shard_map/dedisperse/pallas_call | solution.py:799
  14.4 2.2 %templates.1 = bf16[16,128,256]{2,1,0:T(8,128)(2,1)} custom-call(f32[32,512]{1,0:T(8,128)S(1)} %get-tuple-element.7.signal_ref, bf16[256,512]{1,0:T(8,128)(2,1)S(1)} %get-tuple-element.8.taps_ref), custom_call_target="tpu_custom_call" | custom-call | tf_op jit(solution)/shard_map/templates/pallas_call | solution.py:869
